TPU v7x, 256 devices: a whole 4x4x8 slice. The times are simulated.
256 devices in a mesh: dp: 16 (over x, y_hi, core), tensor: 16 (over y_lo, z).
Axes of the slice: x: 4, y: 4 (y_hi: 2, y_lo: 2; y = y_hi * 2 + y_lo), z: 8, core: 2. Of those that a mesh axis runs over, the one named last changes fastest.
Arguments:
- inputs: bfloat16 [8192, 6144], P(('dp', 'tensor')), may hold values from -36 to 36
- gain: float32 [6144], replicated, may hold values from 0.25 to 1.75
- w_in: bfloat16 [6144, 12288], P(None, 'tensor'), may hold values from -0.078125 to 0.078125
- grad_act: bfloat16 [8192, 12288], P('dp', 'tensor'), may hold values from -6 to 6
- residual_gradient: bfloat16 [8192, 6144], P(('dp', 'tensor')), may hold values from -6 to 6
Outputs:
- block_input_gradient: bfloat16 [8192, 6144], P(('dp', 'tensor'))
- grad_w: float32 [6144, 12288], P('dp', 'tensor')
- scale_gradient: float32 [6144], replicated
All inputs are finite; a program needn't handle non-finite values.
Results may differ from a plain program's by a relative error of at most 0.022.
Values may be sent and summed in bfloat16 or wider, within the bound.
No kernel may reach another device: no remote copies, remote signals or barrier semaphores. Data moves between devices by JAX's collectives and lax.ppermute only.
A program may use at most 128 MiB of HBM per device.

v0:
```python
import jax
import jax.numpy as jnp
from jax import lax
from jax.sharding import PartitionSpec as P


def contract_rows(left, right):
    return lax.dot_general(
        left, right, (((0,), (0,)), ((), ())), preferred_element_type=jnp.float32
    )


def on_device(inputs, gain, w_in, grad_act, residual_gradient):
    values = inputs.astype(jnp.float32)
    centered_input = values - jnp.mean(values, axis=1, keepdims=True)
    inverse_deviation = lax.rsqrt(
        jnp.mean(centered_input * centered_input, axis=1, keepdims=True) + 1e-06
    )
    standardized_input = centered_input * inverse_deviation
    normed_output = (standardized_input * gain).astype(jnp.bfloat16)
    replicas = lax.axis_size("dp")
    full = lax.all_gather(normed_output, "tensor", axis=0, tiled=True)
    pre = jnp.dot(full, w_in, preferred_element_type=jnp.float32)
    unused, pullback = jax.vjp(jax.nn.gelu, pre)
    dpre = pullback(grad_act.astype(jnp.float32))[0].astype(jnp.bfloat16)
    normed_gradient = lax.psum_scatter(
        lax.dot_general(
            dpre, w_in, (((1,), (1,)), ((), ())), preferred_element_type=jnp.float32
        ).astype(jnp.bfloat16),
        "tensor",
        scatter_dimension=0,
        tiled=True,
    ).astype(jnp.float32)
    scale_terms = jnp.sum(normed_gradient * standardized_input, axis=0)
    scale_gradient = lax.psum(scale_terms, ("dp", "tensor")) / replicas
    scaled_gradient = normed_gradient * gain
    first_average = jnp.mean(scaled_gradient, axis=1, keepdims=True)
    second_average = jnp.mean(scaled_gradient * standardized_input, axis=1, keepdims=True)
    block_input_gradient = (
        residual_gradient.astype(jnp.float32)
        + inverse_deviation
        * (scaled_gradient - first_average - standardized_input * second_average)
    ).astype(jnp.bfloat16)
    term = contract_rows(full, dpre)
    grad_w = (
        lax.psum_scatter(term.astype(jnp.bfloat16), "dp", scatter_dimension=0, tiled=True).astype(
            jnp.float32
        )
        / replicas
    )
    return (block_input_gradient, grad_w, scale_gradient)


def solution(mesh):
    return jax.shard_map(
        on_device,
        mesh=mesh,
        in_specs=(
            P(("dp", "tensor"), None),
            P(),
            P(None, "tensor"),
            P("dp", "tensor"),
            P(("dp", "tensor"), None),
        ),
        out_specs=(P(("dp", "tensor"), None), P("dp", "tensor"), P()),
        check_vma=False,
    )
```

profile of v0, /device:TPU:2, one launch (start us, length us, event | category | flops | bytes accessed | tf_op | source)
XLA Modules:
  0.0 327.8 jit_solution(12556771568084619879)
XLA Ops:
  7.2 0.0 all-gather.2.cloned.1.call-start
  7.2 1.2 convert_reduce_fusion
  8.4 1.3 fusion.24
  9.7 1.9 fusion.19
  11.6 0.0 all-gather.2.cloned.1.call-update
  11.6 0.0 copy-start.3
  11.6 0.0 reduce-scatter.3.cloned.1.call-start
  11.7 85.2 %all-gather.2.cloned.1.call-done = bf16[512,6144]{1,0:T(8,128)(2,1)} async-done(((bf16[32,6144]{1,0:T(8,128)(2,1)}), bf16[512,6144]{1,0:T(8,128)(2,1)}) %all-gather.2.cloned.1.call-update) | async-done | bytes 6291472 | tf_op jit(solution)/shard_map/all_gather | solution.py:22
  96.9 9.4 %fusion.51 = f32[512,768]{1,0:T(8,128)S(1)} fusion(bf16[512,6144]{1,0:T(8,128)(2,1)} %all-gather.2.cloned.1.call-done, bf16[6144,768]{1,0:T(8,128)(2,1)} %param.7), kind=kOutput, calls=%fused_computation.65 | convolution fusion | flops 4831838208 | bytes 17301504 | tf_op jit(solution)/shard_map/dot_general | solution.py:23
  106.3 0.0 copy-done.3
  106.3 11.4 %convolution_convert_fusion.1 = bf16[512,6144]{1,0:T(8,128)(2,1)} fusion(bf16[6144,768]{1,0:T(8,128)(2,1)} %param.7, bf16[512,768]{1,0:T(8,128)(2,1)S(1)} %copy-done.3, f32[512,768]{1,0:T(8,128)S(1)} %fusion.51), kind=kOutput, calls=%fused_computation.1 | convolution fusion | flops 4843241472 | bytes 18087936 | tf_op jit(solution)/shard_map/dot_general | solution.py:27
  117.7 0.0 reduce-scatter.3.cloned.1.call-update
  117.7 0.0 reduce-scatter.5.cloned.1.call-start
  117.8 11.3 %convolution_convert_fusion = bf16[6144,768]{1,0:T(8,128)(2,1)} fusion(bf16[512,6144]{1,0:T(8,128)(2,1)} %all-gather.2.cloned.1.call-done, bf16[512,768]{1,0:T(8,128)(2,1)S(1)} %copy-done.3, f32[512,768]{1,0:T(8,128)S(1)} %fusion.51), kind=kOutput, calls=%fused_computation | convolution fusion | flops 4844814336 | bytes 18087936 | tf_op jit(solution)/shard_map/dot_general | solution.py:8
  129.0 0.0 reduce-scatter.5.cloned.1.call-update
  129.1 73.0 %reduce-scatter.3.cloned.1.call-done = bf16[32,6144]{1,0:T(8,128)(2,1)} async-done(((bf16[512,6144]{1,0:T(8,128)(2,1)}), bf16[32,6144]{1,0:T(8,128)(2,1)}) %reduce-scatter.3.cloned.1.call-update) | async-done | bytes 393232 | tf_op jit(solution)/shard_map/reduce_scatter | solution.py:26
  202.1 0.0 copy-done
  202.1 0.0 copy-done.2
  202.1 1.5 fusion.26
  203.6 83.6 %psum.7 = f32[6144]{0:T(1024)S(1)} all-reduce(f32[6144]{0:T(1024)S(1)} %get-tuple-element.3), channel_id=1, replica_groups=mesh['dp'=16,'tensor'=16] {'dp','tensor'}, use_global_device_ids=true, to_apply=%region_7.0 | all-reduce | flops 6144 | bytes 49152 | tf_op jit(solution)/shard_map/psum | solution.py:35
  287.1 0.6 broadcast_multiply_fusion
  287.8 2.1 fusion.23
  289.9 29.3 %reduce-scatter.5.cloned.1.call-done = bf16[384,768]{1,0:T(8,128)(2,1)} async-done(((bf16[6144,768]{1,0:T(8,128)(2,1)}), bf16[384,768]{1,0:T(8,128)(2,1)}) %reduce-scatter.5.cloned.1.call-update) | async-done | bytes 589840 | tf_op jit(solution)/shard_map/reduce_scatter | solution.py:46
  319.2 2.2 convert_multiply_fusion.2
  (7 shorter events, 0.0 us)
Async XLA Ops:
  7.2 89.8 %all-gather.2.cloned.1.call-start = ((), (), s32[]{:S(2)}) async-start(), calls=%async_computation.2 | async-start | bytes 6684672 | tf_op jit(solution)/shard_map/all_gather | solution.py:22
  11.6 94.7 %copy-start.3 = (bf16[512,768]{1,0:T(8,128)(2,1)S(1)}, bf16[512,768]{1,0:T(8,128)(2,1)}, u32[]{:S(2)}) copy-start(bf16[512,768]{1,0:T(8,128)(2,1)} %param.8) | copy-start | bytes 2359300
  11.6 190.5 %reduce-scatter.3.cloned.1.call-start = ((), (), s32[]{:S(2)}) async-start(), calls=%async_computation.3 | async-start | bytes 6684672 | tf_op jit(solution)/shard_map/reduce_scatter | solution.py:26
  117.7 201.4 %reduce-scatter.5.cloned.1.call-start = ((), (), s32[]{:S(2)}) async-start(), calls=%async_computation.4 | async-start | bytes 10027008 | tf_op jit(solution)/shard_map/reduce_scatter | solution.py:46
  129.0 73.1 %copy-start = (bf16[32,6144]{1,0:T(8,128)(2,1)S(1)}, bf16[32,6144]{1,0:T(8,128)(2,1)}, u32[]{:S(2)}) copy-start(bf16[32,6144]{1,0:T(8,128)(2,1)} %param.5) | copy-start | bytes 1179652
  129.0 73.1 %copy-start.2 = (f32[6144]{0:T(1024)S(1)}, f32[6144]{0:T(1024)}, u32[]{:S(2)}) copy-start(f32[6144]{0:T(1024)} %param.6) | copy-start | bytes 73732
  129.0 158.7 %copy-start.1 = (bf16[32,6144]{1,0:T(8,128)(2,1)S(1)}, bf16[32,6144]{1,0:T(8,128)(2,1)}, u32[]{:S(2)}) copy-start(bf16[32,6144]{1,0:T(8,128)(2,1)} %param.9) | copy-start | bytes 1179652
Sparse Core Ops, SparseCore 0:
  11.7 85.1 all-gather.1
  117.8 84.2 reduce-scatter.2
  206.8 112.2 reduce-scatter.4
where the time goes:
time: 328 us
  waiting for transfers between devices  188 us (57%)
  blocking collectives  83.6 us (25%)
  matrix products  32 us (10%)
  between operations  13.8 us (4%)
  other arithmetic  10.7 us (3%)
    all_gather x1, waiting for transfers between devices, on_device(): full = lax.all_gather(normed_output, 'tensor', axis=0, tiled=True)  85.2 us
    psum x1, blocking collectives, on_device(): scale_gradient = lax.psum(scale_terms, ('dp', 'tensor')) / replicas  83.6 us
    reduce_scatter x1, waiting for transfers between devices, on_device(): lax.psum_scatter(lax.dot_general(dpre, w_in, (((1,), (1,)), ((), ())), pr...  73 us
    reduce_scatter x1, waiting for transfers between devices, on_device(): lax.psum_scatter(term.astype(jnp.bfloat16), 'dp', scatter_dimension=0, ti...  29.3 us
    dot_general x1, matrix products, on_device(): lax.dot_general(dpre, w_in, (((1,), (1,)), ((), ())), preferred_element_t...  11.4 us
    dot_general x1, matrix products, contract_rows(): lax.dot_general(left, right, (((0,), (0,)), ((), ())), preferred_element_...  11.3 us
    dot_general x1, matrix products, on_device(): pre = jnp.dot(full, w_in, preferred_element_type=jnp.float32)  9.35 us
  transfers between devices with their start and end apart: 3, of which 3 were waited for; matrix products, arithmetic and copies ran while one was open for 5% of the time, Pallas kernels for 0%

commit v1 on v0

--- a/solution.py
+++ b/solution.py
@@ -2,6 +2,11 @@
 import jax.numpy as jnp
 from jax import lax
 from jax.sharding import PartitionSpec as P
+
+
+def gather_over(value, mesh_axis, dim):
+    sent = jnp.stack([value] * lax.axis_size(mesh_axis))
+    return jnp.concatenate(lax.all_to_all(sent, mesh_axis, 0, 0), axis=dim)
 
 
 def contract_rows(left, right):
@@ -19,7 +24,7 @@
     standardized_input = centered_input * inverse_deviation
     normed_output = (standardized_input * gain).astype(jnp.bfloat16)
     replicas = lax.axis_size("dp")
-    full = lax.all_gather(normed_output, "tensor", axis=0, tiled=True)
+    full = gather_over(normed_output, "tensor", 0)
     pre = jnp.dot(full, w_in, preferred_element_type=jnp.float32)
     unused, pullback = jax.vjp(jax.nn.gelu, pre)
     dpre = pullback(grad_act.astype(jnp.float32))[0].astype(jnp.bfloat16)

time: 328 us -> 388 us (1.18)
  blocking collectives: 83.6 us -> 232 us
  waiting for transfers between devices: 188 us -> 103 us
  matrix products: 32 us -> 24.9 us
    all_to_all x0 -> x1, blocking collectives: none -> 149 us  [gather_over(): return jnp.concatenate(lax.all_to_all(sent, mesh_axis, 0, 0), axis=dim)]
    all_gather x1 -> x0, waiting for transfers between devices: 85.2 us -> none  [on_device(): full = lax.all_gather(normed_output, 'tensor', axis=0, tiled=True)]
    dot_general x1, matrix products: 9.35 us -> 5.06 us  [on_device(): pre = jnp.dot(full, w_in, preferred_element_type=jnp.float32)]
  transfers between devices with their start and end apart: 3 -> 2, of which waited for: 3 -> 2; matrix products, arithmetic and copies ran while one was open for 5% -> 4% of each run, Pallas kernels for 0% -> 0%
where the time goes in v1:
time: 388 us
  blocking collectives  232 us (60%)
  waiting for transfers between devices  103 us (27%)
  matrix products  24.9 us (6%)
  between operations  14.1 us (4%)
  other arithmetic  9.94 us (3%)
    all_to_all x1, blocking collectives, gather_over(): return jnp.concatenate(lax.all_to_all(sent, mesh_axis, 0, 0), axis=dim)  149 us
    psum x1, blocking collectives, on_device(): scale_gradient = lax.psum(scale_terms, ('dp', 'tensor')) / replicas  83.1 us
    reduce_scatter x1, waiting for transfers between devices, on_device(): lax.psum_scatter(lax.dot_general(dpre, w_in, (((1,), (1,)), ((), ())), pr...  73.7 us
    reduce_scatter x1, waiting for transfers between devices, on_device(): lax.psum_scatter(term.astype(jnp.bfloat16), 'dp', scatter_dimension=0, ti...  29.7 us
    dot_general x1, matrix products, contract_rows(): lax.dot_general(left, right, (((0,), (0,)), ((), ())), preferred_element_...  11.3 us
    dot_general x1, matrix products, on_device(): lax.dot_general(dpre, w_in, (((1,), (1,)), ((), ())), preferred_element_t...  8.52 us
  transfers between devices with their start and end apart: 2, of which 2 were waited for; matrix products, arithmetic and copies ran while one was open for 4% of the time, Pallas kernels for 0%

profile of v1, /device:TPU:2, one launch (start us, length us, event | category | flops | bytes accessed | tf_op | source)
XLA Modules:
  0.0 387.9 jit_solution(17176431420358329965)
XLA Ops:
  7.2 0.0 reduce-scatter.3.cloned.1.call-start
  7.2 1.2 convert_reduce_fusion
  8.4 1.3 fusion.24
  9.7 1.2 fusion.19
  10.9 0.0 slice-start
  10.9 0.0 slice-start.1
  10.9 0.8 stack.2
  11.6 0.0 slice-start.2
  11.7 148.9 %all_to_all.5 = bf16[16,32,6144]{2,1,0:T(8,128)(2,1)S(1)} all-to-all(bf16[16,32,6144]{2,1,0:T(8,128)(2,1)S(1)} %stack.2), channel_id=1, replica_groups=mesh['dp'=16,'tensor'=16] {'tensor'}, dimensions={0} | all-to-all | bytes 12582912 | tf_op jit(solution)/shard_map/all_to_all | solution.py:9
  160.6 2.6 copy-done.1
  163.2 0.0 copy-start.4
  163.2 5.1 %fusion.51 = f32[512,768]{1,0:T(8,128)S(1)} fusion(bf16[512,6144]{1,0:T(8,128)(2,1)S(1)} %bitcast.5, bf16[6144,768]{1,0:T(8,128)(2,1)S(1)} %bitcast.8), kind=kOutput, calls=%fused_computation.65 | convolution fusion | flops 4831838208 | bytes 17301504 | tf_op jit(solution)/shard_map/dot_general | solution.py:28
  168.3 8.5 %convolution_convert_fusion.1 = bf16[512,6144]{1,0:T(8,128)(2,1)} fusion(bf16[6144,768]{1,0:T(8,128)(2,1)S(1)} %bitcast.8, bf16[512,768]{1,0:T(8,128)(2,1)S(1)} %copy-done.4, f32[512,768]{1,0:T(8,128)S(1)} %fusion.51), kind=kOutput, calls=%fused_computation.1 | convolution fusion | flops 4843241472 | bytes 18087936 | tf_op jit(solution)/shard_map/dot_general | solution.py:32
  176.8 0.0 reduce-scatter.3.cloned.1.call-update
  176.9 0.0 reduce-scatter.5.cloned.1.call-start
  176.9 11.3 %convolution_convert_fusion = bf16[6144,768]{1,0:T(8,128)(2,1)} fusion(bf16[512,6144]{1,0:T(8,128)(2,1)} %bitcast.6, bf16[512,768]{1,0:T(8,128)(2,1)S(1)} %copy-done.4, f32[512,768]{1,0:T(8,128)S(1)} %fusion.51), kind=kOutput, calls=%fused_computation | convolution fusion | flops 4844814336 | bytes 18087936 | tf_op jit(solution)/shard_map/dot_general | solution.py:13
  188.2 0.0 reduce-scatter.5.cloned.1.call-update
  188.2 73.7 %reduce-scatter.3.cloned.1.call-done = bf16[32,6144]{1,0:T(8,128)(2,1)} async-done(((bf16[512,6144]{1,0:T(8,128)(2,1)}), bf16[32,6144]{1,0:T(8,128)(2,1)}) %reduce-scatter.3.cloned.1.call-update) | async-done | bytes 393232 | tf_op jit(solution)/shard_map/reduce_scatter | solution.py:31
  261.9 1.5 fusion.26
  263.4 83.1 %psum.7 = f32[6144]{0:T(1024)S(1)} all-reduce(f32[6144]{0:T(1024)S(1)} %get-tuple-element.3), channel_id=1, replica_groups=mesh['dp'=16,'tensor'=16] {'dp','tensor'}, use_global_device_ids=true, to_apply=%region_7.0 | all-reduce | flops 6144 | bytes 49152 | tf_op jit(solution)/shard_map/psum | solution.py:40
  346.5 0.6 broadcast_multiply_fusion
  347.1 2.1 fusion.23
  349.2 29.7 %reduce-scatter.5.cloned.1.call-done = bf16[384,768]{1,0:T(8,128)(2,1)} async-done(((bf16[6144,768]{1,0:T(8,128)(2,1)}), bf16[384,768]{1,0:T(8,128)(2,1)}) %reduce-scatter.5.cloned.1.call-update) | async-done | bytes 589840 | tf_op jit(solution)/shard_map/reduce_scatter | solution.py:51
  378.9 2.2 convert_multiply_fusion.2
  (15 shorter events, 0.0 us)
Async XLA Ops:
  7.2 254.8 %reduce-scatter.3.cloned.1.call-start = ((), (), s32[]{:S(2)}) async-start(), calls=%async_computation.3 | async-start | bytes 6684672 | tf_op jit(solution)/shard_map/reduce_scatter | solution.py:31
  10.9 152.4 %slice-start = ((s8[9437184]{0:T(1024)(128)(4,1)}), s8[4194304]{0:T(1024)(128)(4,1)S(1)}, s32[]{:S(2)}) async-start(s8[9437184]{0:T(1024)(128)(4,1)} %bitcast.7), calls=%async_computation.5 | async-start | bytes 8388608
  10.9 152.4 %slice-start.1 = ((s8[9437184]{0:T(1024)(128)(4,1)}), s8[4194304]{0:T(1024)(128)(4,1)S(1)}, s32[]{:S(2)}) async-start(s8[9437184]{0:T(1024)(128)(4,1)} %bitcast.7), calls=%async_computation.6 | async-start | bytes 8388608
  11.6 151.6 %slice-start.2 = ((s8[9437184]{0:T(1024)(128)(4,1)}), s8[1048576]{0:T(1024)(128)(4,1)S(1)}, s32[]{:S(2)}) async-start(s8[9437184]{0:T(1024)(128)(4,1)} %bitcast.7), calls=%async_computation.7 | async-start | bytes 2097152
  160.6 2.6 copy-start.1
  163.2 5.1 %copy-start.4 = (bf16[512,768]{1,0:T(8,128)(2,1)S(1)}, bf16[512,768]{1,0:T(8,128)(2,1)}, u32[]{:S(2)}) copy-start(bf16[512,768]{1,0:T(8,128)(2,1)} %param.8) | copy-start | bytes 2359300
  176.9 202.0 %reduce-scatter.5.cloned.1.call-start = ((), (), s32[]{:S(2)}) async-start(), calls=%async_computation.4 | async-start | bytes 10027008 | tf_op jit(solution)/shard_map/reduce_scatter | solution.py:51
  188.2 73.7 %copy-start = (bf16[32,6144]{1,0:T(8,128)(2,1)S(1)}, bf16[32,6144]{1,0:T(8,128)(2,1)}, u32[]{:S(2)}) copy-start(bf16[32,6144]{1,0:T(8,128)(2,1)} %param.5) | copy-start | bytes 1179652
  188.2 73.7 %copy-start.3 = (f32[6144]{0:T(1024)S(1)}, f32[6144]{0:T(1024)}, u32[]{:S(2)}) copy-start(f32[6144]{0:T(1024)} %param.6) | copy-start | bytes 73732
  188.2 158.9 %copy-start.2 = (bf16[32,6144]{1,0:T(8,128)(2,1)S(1)}, bf16[32,6144]{1,0:T(8,128)(2,1)}, u32[]{:S(2)}) copy-start(bf16[32,6144]{1,0:T(8,128)(2,1)} %param.9) | copy-start | bytes 1179652
Sparse Core Ops, SparseCore 0:
  177.0 84.8 reduce-scatter.2
  266.6 112.2 reduce-scatter.4

commit v2 on v0

--- a/solution.py
+++ b/solution.py
@@ -32,7 +32,8 @@
         tiled=True,
     ).astype(jnp.float32)
     scale_terms = jnp.sum(normed_gradient * standardized_input, axis=0)
-    scale_gradient = lax.psum(scale_terms, ("dp", "tensor")) / replicas
+    fix_inputs_on = lambda z_in: jnp.sum(lax.all_gather(z_in, axis_name=("dp", "tensor")), 0)
+    scale_gradient = fix_inputs_on(scale_terms) / replicas
     scaled_gradient = normed_gradient * gain
     first_average = jnp.mean(scaled_gradient, axis=1, keepdims=True)
     second_average = jnp.mean(scaled_gradient * standardized_input, axis=1, keepdims=True)

time: 328 us -> 1060 us (3.23)
  waiting for transfers between devices: 188 us -> 982 us
  blocking collectives: 83.6 us -> 0 us
    all_gather x0 -> x1, waiting for transfers between devices: none -> 712 us  [on_device(): lax.all_gather(z_in, axis_name=('dp', 'tensor'))]
    psum x1 -> x0, blocking collectives: 83.6 us -> none  [on_device(): scale_gradient = lax.psum(scale_terms, ('dp', 'tensor')) / replicas]
    reduce_scatter x1, waiting for transfers between devices: 29.3 us -> 112 us  [on_device(): lax.psum_scatter(term.astype(jnp.bfloat16), 'dp', scatter_dimension=0, ti...]
  transfers between devices with their start and end apart: 3 -> 4, of which waited for: 3 -> 4; matrix products, arithmetic and copies ran while one was open for 5% -> 2% of each run, Pallas kernels for 0% -> 0%
where the time goes in v2:
time: 1060 us; the launch traced here: 1050 us
  waiting for transfers between devices  982 us (93%)
  matrix products  32 us (3%)
  other arithmetic  14.3 us (1%)
  between operations  13.8 us (1%)
    all_gather x1, waiting for transfers between devices, on_device(): lax.all_gather(z_in, axis_name=('dp', 'tensor'))  712 us
    reduce_scatter x1, waiting for transfers between devices, on_device(): lax.psum_scatter(term.astype(jnp.bfloat16), 'dp', scatter_dimension=0, ti...  112 us
    all_gather x1, waiting for transfers between devices, on_device(): full = lax.all_gather(normed_output, 'tensor', axis=0, tiled=True)  85.2 us
    reduce_scatter x1, waiting for transfers between devices, on_device(): lax.psum_scatter(lax.dot_general(dpre, w_in, (((1,), (1,)), ((), ())), pr...  72.9 us
  transfers between devices with their start and end apart: 4, of which 4 were waited for; matrix products, arithmetic and copies ran while one was open for 2% of the time, Pallas kernels for 0%

profile of v2, /device:TPU:2, one launch (start us, length us, event | category | flops | bytes accessed | tf_op | source)
XLA Modules:
  0.0 1049.9 jit_solution(13652629415884180098)
XLA Ops:
  7.2 0.0 all-gather.4.cloned.1.call-start
  7.2 1.2 convert_reduce_fusion
  8.4 1.3 fusion.24
  9.7 1.9 fusion.19
  11.6 0.0 all-gather.4.cloned.1.call-update
  11.6 0.0 reduce-scatter.3.cloned.1.call-start
  11.7 85.2 %all-gather.4.cloned.1.call-done = bf16[512,6144]{1,0:T(8,128)(2,1)} async-done(((bf16[32,6144]{1,0:T(8,128)(2,1)}), bf16[512,6144]{1,0:T(8,128)(2,1)}) %all-gather.4.cloned.1.call-update) | async-done | bytes 6291472 | tf_op jit(solution)/shard_map/all_gather | solution.py:22
  96.9 9.3 fusion.51
  106.3 11.4 %convolution_convert_fusion.1 = bf16[512,6144]{1,0:T(8,128)(2,1)} fusion(bf16[6144,768]{1,0:T(8,128)(2,1)} %param.7, bf16[512,768]{1,0:T(8,128)(2,1)S(1)} %copy-done.3, f32[512,768]{1,0:T(8,128)S(1)} %fusion.51), kind=kOutput, calls=%fused_computation.1 | convolution fusion | flops 4843241472 | bytes 18087936 | tf_op jit(solution)/shard_map/dot_general | solution.py:27
  117.7 0.0 reduce-scatter.3.cloned.1.call-update
  117.7 0.0 reduce-scatter.5.cloned.1.call-start
  117.7 11.3 %convolution_convert_fusion = bf16[6144,768]{1,0:T(8,128)(2,1)} fusion(bf16[512,6144]{1,0:T(8,128)(2,1)} %all-gather.4.cloned.1.call-done, bf16[512,768]{1,0:T(8,128)(2,1)S(1)} %copy-done.3, f32[512,768]{1,0:T(8,128)S(1)} %fusion.51), kind=kOutput, calls=%fused_computation | convolution fusion | flops 4844814336 | bytes 18087936 | tf_op jit(solution)/shard_map/dot_general | solution.py:8
  129.0 0.0 reduce-scatter.5.cloned.1.call-update
  129.1 0.0 all-gather.6.cloned.1.call-start
  129.1 72.9 %reduce-scatter.3.cloned.1.call-done = bf16[32,6144]{1,0:T(8,128)(2,1)} async-done(((bf16[512,6144]{1,0:T(8,128)(2,1)}), bf16[32,6144]{1,0:T(8,128)(2,1)}) %reduce-scatter.3.cloned.1.call-update) | async-done | bytes 393232 | tf_op jit(solution)/shard_map/reduce_scatter | solution.py:26
  202.0 2.0 fusion.26
  204.0 0.0 all-gather.6.cloned.1.call-update
  204.0 2.1 fusion.23
  206.1 112.4 %reduce-scatter.5.cloned.1.call-done = bf16[384,768]{1,0:T(8,128)(2,1)} async-done(((bf16[6144,768]{1,0:T(8,128)(2,1)}), bf16[384,768]{1,0:T(8,128)(2,1)}) %reduce-scatter.5.cloned.1.call-update) | async-done | bytes 589840 | tf_op jit(solution)/shard_map/reduce_scatter | solution.py:47
  318.5 2.2 convert_multiply_fusion.2
  320.7 711.7 %all-gather.6.cloned.1.call-done = f32[1572864]{0:T(1024)} async-done(((f32[6144]{0:T(1024)}), f32[1572864]{0:T(1024)}) %all-gather.6.cloned.1.call-update) | async-done | bytes 6291472 | tf_op jit(solution)/shard_map/all_gather | solution.py:35
  1032.3 7.3 reshape.27
  1039.7 3.1 reduce_sum.59
  1042.8 0.6 broadcast_multiply_fusion
  (11 shorter events, 0.0 us)
Async XLA Ops:
  7.2 89.8 %all-gather.4.cloned.1.call-start = ((), (), s32[]{:S(2)}) async-start(), calls=%async_computation.2 | async-start | bytes 6684672 | tf_op jit(solution)/shard_map/all_gather | solution.py:22
  11.6 94.6 %copy-start.3 = (bf16[512,768]{1,0:T(8,128)(2,1)S(1)}, bf16[512,768]{1,0:T(8,128)(2,1)}, u32[]{:S(2)}) copy-start(bf16[512,768]{1,0:T(8,128)(2,1)} %param.8) | copy-start | bytes 2359300
  11.6 190.4 %reduce-scatter.3.cloned.1.call-start = ((), (), s32[]{:S(2)}) async-start(), calls=%async_computation.3 | async-start | bytes 6684672 | tf_op jit(solution)/shard_map/reduce_scatter | solution.py:26
  117.7 200.8 %reduce-scatter.5.cloned.1.call-start = ((), (), s32[]{:S(2)}) async-start(), calls=%async_computation.4 | async-start | bytes 10027008 | tf_op jit(solution)/shard_map/reduce_scatter | solution.py:47
  129.0 73.0 %copy-start = (bf16[32,6144]{1,0:T(8,128)(2,1)S(1)}, bf16[32,6144]{1,0:T(8,128)(2,1)}, u32[]{:S(2)}) copy-start(bf16[32,6144]{1,0:T(8,128)(2,1)} %param.5) | copy-start | bytes 1179652
  129.0 73.0 %copy-start.2 = (f32[6144]{0:T(1024)S(1)}, f32[6144]{0:T(1024)}, u32[]{:S(2)}) copy-start(f32[6144]{0:T(1024)} %param.6) | copy-start | bytes 73732
  129.0 75.0 %copy-start.1 = (bf16[32,6144]{1,0:T(8,128)(2,1)S(1)}, bf16[32,6144]{1,0:T(8,128)(2,1)}, u32[]{:S(2)}) copy-start(bf16[32,6144]{1,0:T(8,128)(2,1)} %param.9) | copy-start | bytes 1179652
  129.1 903.3 %all-gather.6.cloned.1.call-start = ((), (), s32[]{:S(2)}) async-start(), calls=%async_computation.5 | async-start | bytes 6316032 | tf_op jit(solution)/shard_map/all_gather | solution.py:35
Sparse Core Ops, SparseCore 0:
  11.7 85.1 all-gather.3
  117.8 84.1 reduce-scatter.2
  206.8 111.7 reduce-scatter.4
  320.8 711.4 all-gather.5
